TPU v7x, 256 devices: a whole 4x4x8 slice. The times are simulated.
256 devices in a mesh: seq: 128 (over z, y, x_lo, core), head: 2 (over x_hi).
Axes of the slice: x: 4 (x_hi: 2, x_lo: 2; x = x_hi * 2 + x_lo), y: 4, z: 8, core: 2. Of those that a mesh axis runs over, the one named last changes fastest.
Arguments:
- queries: bfloat16 [32768, 4096], P('seq', 'head'), may hold values from -8 to 8
- keys: bfloat16 [32768, 2048], P('seq', 'head'), may hold values from -8 to 8
- values: bfloat16 [32768, 2048], P('seq', 'head'), may hold values from -6 to 6
- segment_ids: int32 [32768], P(('seq', 'head')), may hold values from 0 to 63, never falling along the last dimension, each value on 1 to 2048 neighbouring positions
Outputs:
- attended: bfloat16 [32768, 4096], P('seq', 'head')
Inputs may be any that keep to these rules, and one draw needn't show every extreme that they name: `segment_ids`: document numbers never fall along the tokens; each document has 1 to 2048 tokens, one exactly 2048.
All inputs are finite; a program needn't handle non-finite values.
Results may differ from a plain program's by a relative error of at most 0.0037.
Values may be sent and summed in bfloat16 or wider, within the bound.
A program may use at most 64 MiB of HBM per device.

v0:
```python
import jax
import jax.numpy as jnp
from jax import lax
from jax.sharding import PartitionSpec as P

HEAD_WIDTH = 128
WINDOW = 1024


score_scale = 168.0 ** (-0.5)


def from_behind(value, axis, steps):
    count = lax.axis_size(axis)
    initial, last = (max(0, -steps), min(count, count - steps))
    return lax.ppermute(value, axis, [(source, source + steps) for source in range(initial, last)])


def attend(queries, keys, values, query_ids, key_ids, query_pos, key_pos):
    tok_rows = queries.shape[0]
    span = keys.shape[0]
    kv_heads = keys.shape[1] // HEAD_WIDTH
    group = queries.shape[1] // keys.shape[1]
    visible = (
        (key_ids[None, :] == query_ids[:, None])
        & (key_pos[None, :] <= query_pos[:, None])
        & (query_pos[:, None] - key_pos[None, :] < WINDOW)
    )
    grouped_q = queries.reshape(tok_rows, kv_heads, group, HEAD_WIDTH).transpose(1, 0, 2, 3)
    grouped_k = keys.reshape(span, kv_heads, HEAD_WIDTH).transpose(1, 0, 2)
    grouped_v = values.reshape(span, kv_heads, HEAD_WIDTH).transpose(1, 0, 2)

    def one_head(operands):
        head_q, head_k, head_v = operands
        scores = (
            jnp.einsum("tgd,sd->gts", head_q, head_k, preferred_element_type=jnp.float32)
            * score_scale
        )
        scores = jnp.where(visible[None], scores, -1e30)
        top = jnp.max(scores, axis=2, keepdims=True)
        weights = jnp.exp(scores - top)
        total = jnp.sum(weights, axis=2)
        rounded = weights.astype(jnp.bfloat16)
        mixed = jnp.einsum("gts,sd->tgd", rounded, head_v, preferred_element_type=jnp.float32)
        return (mixed / total.T[:, :, None]).astype(jnp.bfloat16)

    final_output = lax.map(one_head, (grouped_q, grouped_k, grouped_v))
    return final_output.transpose(1, 0, 2, 3).reshape(tok_rows, -1)


def body(queries, keys, values, segment_ids):
    own_ids = lax.all_gather(segment_ids, "head", axis=0, tiled=True)
    tok_rows = keys.shape[0]
    reach = WINDOW // tok_rows
    tagged = own_ids + 1
    packet = (keys, values, tagged)
    received = []
    for distance in range(reach):
        received.append(from_behind((packet[0], packet[1], packet[2]), "seq", distance + 1))
    ordered = list(reversed(received)) + [packet]
    all_keys = jnp.concatenate([piece[0] for piece in ordered], axis=0)
    all_values = jnp.concatenate([piece[1] for piece in ordered], axis=0)
    key_ids = jnp.concatenate([piece[2] for piece in ordered], axis=0) - 1
    query_pos = jnp.arange(tok_rows, dtype=jnp.int32)
    key_pos = jnp.arange(all_keys.shape[0], dtype=jnp.int32) - reach * tok_rows
    return attend(queries, all_keys, all_values, own_ids, key_ids, query_pos, key_pos)


def solution(mesh):
    in_specs = (P("seq", "head"), P("seq", "head"), P("seq", "head"), P(("seq", "head")))
    out_specs = P("seq", "head")
    return jax.shard_map(body, mesh=mesh, in_specs=in_specs, out_specs=out_specs, check_vma=False)
```

profile of v0, /device:TPU:132, one launch (start us, length us, event | category | flops | bytes accessed | tf_op | source)
XLA Modules:
  0.0 159.4 jit_solution(14425892911807123845)
XLA Ops:
  0.0 6.0 %all-gather = s32[2,1,128]{2,1,0:T(1,128)S(1)} all-gather(s32[1,1,128]{2,1,0:T(1,128)} %bitcast.69), channel_id=1, replica_groups=mesh['seq'=128,'head'=2] {'head'}, dimensions={0}, use_global_device_ids=true | all-gather | bytes 1536 | tf_op jit(solution)/shard_map/all_gather | solution.py:52
  6.0 3.5 %collective-permute-start.4 = (s32[256]{0:T(256)S(1)}, s32[256]{0:T(256)S(1)}, u32[]{:S(2)}, u32[]{:S(2)}) collective-permute-start(s32[256]{0:T(256)S(1)} %broadcast_add_fusion.1), channel_id=1, source_target_pairs={{0,8},{2,10},{4,12},{6,14},{8,16},{10,18},{12,20},{14,22},{16,24},... | collective-permute-start | bytes 3080 | tf_op jit(solution)/shard_map/ppermute | solution.py:16
  9.5 1.9 %collective-permute-start.5 = (s32[256]{0:T(256)S(1)}, s32[256]{0:T(256)S(1)}, u32[]{:S(2)}, u32[]{:S(2)}) collective-permute-start(s32[256]{0:T(256)S(1)} %broadcast_add_fusion.1), channel_id=1, source_target_pairs={{0,6},{2,8},{4,10},{6,12},{8,14},{10,16},{12,18},{14,20},{16,22},{... | collective-permute-start | bytes 3080 | tf_op jit(solution)/shard_map/ppermute | solution.py:16
  11.4 3.1 %collective-permute-start.6 = (s32[256]{0:T(256)S(1)}, s32[256]{0:T(256)S(1)}, u32[]{:S(2)}, u32[]{:S(2)}) collective-permute-start(s32[256]{0:T(256)S(1)} %broadcast_add_fusion.1), channel_id=1, source_target_pairs={{0,4},{2,6},{4,8},{6,10},{8,12},{10,14},{12,16},{14,18},{16,20},{1... | collective-permute-start | bytes 3080 | tf_op jit(solution)/shard_map/ppermute | solution.py:16
  14.5 3.3 %collective-permute-start.7 = (s32[256]{0:T(256)S(1)}, s32[256]{0:T(256)S(1)}, u32[]{:S(2)}, u32[]{:S(2)}) collective-permute-start(s32[256]{0:T(256)S(1)} %broadcast_add_fusion.1), channel_id=1, source_target_pairs={{0,2},{2,4},{4,6},{6,8},{8,10},{10,12},{12,14},{14,16},{16,18},{18... | collective-permute-start | bytes 3080 | tf_op jit(solution)/shard_map/ppermute | solution.py:16
  17.8 1.2 copy.21
  19.1 3.2 %collective-permute-start.8 = (bf16[256,1024]{0,1:T(8,128)(2,1)S(1)}, bf16[256,1024]{0,1:T(8,128)(2,1)S(1)}, u32[]{:S(2)}, u32[]{:S(2)}) collective-permute-start(bf16[256,1024]{0,1:T(8,128)(2,1)S(1)} %copy.21), channel_id=1, source_target_pairs={{0,8},{2,10},{4,12},{6,14},{8,16},{10,18},{12,20},{14,22},{16,24},... | collective-permute-start | bytes 1572872 | tf_op jit(solution)/shard_map/ppermute | solution.py:16
  22.3 2.3 %copy.26 = bf16[256,2048]{0,1:T(8,128)(2,1)} copy(bf16[256,2048]{1,0:T(8,128)(2,1)} %param.6) | data formatting | bytes 2097152 | tf_op args[0]
  24.6 3.0 %collective-permute-start.9 = (bf16[256,1024]{0,1:T(8,128)(2,1)S(1)}, bf16[256,1024]{0,1:T(8,128)(2,1)S(1)}, u32[]{:S(2)}, u32[]{:S(2)}) collective-permute-start(bf16[256,1024]{0,1:T(8,128)(2,1)S(1)} %copy.21), channel_id=1, source_target_pairs={{0,6},{2,8},{4,10},{6,12},{8,14},{10,16},{12,18},{14,20},{16,22},{... | collective-permute-start | bytes 1572872 | tf_op jit(solution)/shard_map/ppermute | solution.py:16
  27.6 2.9 %collective-permute-start.10 = (bf16[256,1024]{0,1:T(8,128)(2,1)S(1)}, bf16[256,1024]{0,1:T(8,128)(2,1)S(1)}, u32[]{:S(2)}, u32[]{:S(2)}) collective-permute-start(bf16[256,1024]{0,1:T(8,128)(2,1)S(1)} %copy.21), channel_id=1, source_target_pairs={{0,4},{2,6},{4,8},{6,10},{8,12},{10,14},{12,16},{14,18},{16,20},{1... | collective-permute-start | bytes 1572872 | tf_op jit(solution)/shard_map/ppermute | solution.py:16
  30.5 2.2 %collective-permute-start.11 = (bf16[256,1024]{0,1:T(8,128)(2,1)S(1)}, bf16[256,1024]{0,1:T(8,128)(2,1)S(1)}, u32[]{:S(2)}, u32[]{:S(2)}) collective-permute-start(bf16[256,1024]{0,1:T(8,128)(2,1)S(1)} %copy.21), channel_id=1, source_target_pairs={{0,2},{2,4},{4,6},{6,8},{8,10},{10,12},{12,14},{14,16},{16,18},{18... | collective-permute-start | bytes 1572872 | tf_op jit(solution)/shard_map/ppermute | solution.py:16
  32.8 3.5 %collective-permute-start = (bf16[256,1024]{1,0:T(8,128)(2,1)S(1)}, bf16[256,1024]{1,0:T(8,128)(2,1)S(1)}, u32[]{:S(2)}, u32[]{:S(2)}) collective-permute-start(bf16[256,1024]{1,0:T(8,128)(2,1)S(1)} %copy-done), channel_id=1, source_target_pairs={{0,8},{2,10},{4,12},{6,14},{8,16},{10,18},{12,20},{14,22},{16,24},... | collective-permute-start | bytes 1572872 | tf_op jit(solution)/shard_map/ppermute | solution.py:16
  36.3 20.8 %collective-permute-done.8 = bf16[256,1024]{0,1:T(8,128)(2,1)S(1)} collective-permute-done((bf16[256,1024]{0,1:T(8,128)(2,1)S(1)}, bf16[256,1024]{0,1:T(8,128)(2,1)S(1)}, u32[]{:S(2)}, u32[]{:S(2)}) %collective-permute-start.8) | collective-permute-done | bytes 524320 | tf_op jit(solution)/shard_map/ppermute | solution.py:16
  57.1 1.9 %collective-permute-start.1 = (bf16[256,1024]{1,0:T(8,128)(2,1)S(1)}, bf16[256,1024]{1,0:T(8,128)(2,1)S(1)}, u32[]{:S(2)}, u32[]{:S(2)}) collective-permute-start(bf16[256,1024]{1,0:T(8,128)(2,1)S(1)} %copy-done), channel_id=1, source_target_pairs={{0,6},{2,8},{4,10},{6,12},{8,14},{10,16},{12,18},{14,20},{16,22},{... | collective-permute-start | bytes 1572872 | tf_op jit(solution)/shard_map/ppermute | solution.py:16
  59.0 4.7 %collective-permute-start.2 = (bf16[256,1024]{1,0:T(8,128)(2,1)S(1)}, bf16[256,1024]{1,0:T(8,128)(2,1)S(1)}, u32[]{:S(2)}, u32[]{:S(2)}) collective-permute-start(bf16[256,1024]{1,0:T(8,128)(2,1)S(1)} %copy-done), channel_id=1, source_target_pairs={{0,4},{2,6},{4,8},{6,10},{8,12},{10,14},{12,16},{14,18},{16,20},{1... | collective-permute-start | bytes 1572872 | tf_op jit(solution)/shard_map/ppermute | solution.py:16
  63.8 14.0 %collective-permute-done.10 = bf16[256,1024]{0,1:T(8,128)(2,1)S(1)} collective-permute-done((bf16[256,1024]{0,1:T(8,128)(2,1)S(1)}, bf16[256,1024]{0,1:T(8,128)(2,1)S(1)}, u32[]{:S(2)}, u32[]{:S(2)}) %collective-permute-start.10) | collective-permute-done | bytes 524320 | tf_op jit(solution)/shard_map/ppermute | solution.py:16
  77.8 1.9 %collective-permute-start.3 = (bf16[256,1024]{1,0:T(8,128)(2,1)S(1)}, bf16[256,1024]{1,0:T(8,128)(2,1)S(1)}, u32[]{:S(2)}, u32[]{:S(2)}) collective-permute-start(bf16[256,1024]{1,0:T(8,128)(2,1)S(1)} %copy-done), channel_id=1, source_target_pairs={{0,2},{2,4},{4,6},{6,8},{8,10},{10,12},{12,14},{14,16},{16,18},{18... | collective-permute-start | bytes 1572872 | tf_op jit(solution)/shard_map/ppermute | solution.py:16
  79.8 4.6 %collective-permute-done.11 = bf16[256,1024]{0,1:T(8,128)(2,1)S(1)} collective-permute-done((bf16[256,1024]{0,1:T(8,128)(2,1)S(1)}, bf16[256,1024]{0,1:T(8,128)(2,1)S(1)}, u32[]{:S(2)}, u32[]{:S(2)}) %collective-permute-start.11) | collective-permute-done | bytes 524320 | tf_op jit(solution)/shard_map/ppermute | solution.py:16
  84.5 0.9 constant_dynamic-update-slice_fusion.4
  86.2 22.1 %collective-permute-done.2 = bf16[256,1024]{1,0:T(8,128)(2,1)S(1)} collective-permute-done((bf16[256,1024]{1,0:T(8,128)(2,1)S(1)}, bf16[256,1024]{1,0:T(8,128)(2,1)S(1)}, u32[]{:S(2)}, u32[]{:S(2)}) %collective-permute-start.2) | collective-permute-done | bytes 524320 | tf_op jit(solution)/shard_map/ppermute | solution.py:16
  109.2 9.7 %collective-permute-done.3 = bf16[256,1024]{1,0:T(8,128)(2,1)S(1)} collective-permute-done((bf16[256,1024]{1,0:T(8,128)(2,1)S(1)}, bf16[256,1024]{1,0:T(8,128)(2,1)S(1)}, u32[]{:S(2)}, u32[]{:S(2)}) %collective-permute-start.3) | collective-permute-done | bytes 524320 | tf_op jit(solution)/shard_map/ppermute | solution.py:16
  120.5 3.0 %copy.20 = bf16[1280,1024]{0,1:T(8,128)(2,1)S(1)} copy(bf16[1280,1024]{1,0:T(8,128)(2,1)} %constant_dynamic-update-slice_fusion) | data formatting | bytes 5242880 | tf_op jit(solution)/shard_map/concatenate | solution.py:62
  123.5 33.7 %while.11 = (s32[]{:T(128)}, bf16[8,256,2,128]{1,3,2,0:T(8,128)(2,1)}, bf16[8,1280,128]{1,2,0:T(8,128)(2,1)S(1)}, bf16[8,1280,128]{1,2,0:T(8,128)(2,1)}, bf16[8,...) while((s32[]{:T(128)}, ...), condition=%wide.region_3.4_spmd.clone, body=%wide.region_0.3_spmd.clone.sunk | while | flops 342227968 | bytes 9460829 | solution.py:47
  123.5 1.0 fusion.43
  124.5 1.6 fusion.44
  126.5 1.2 fusion.46
  127.7 1.0 fusion.43
  128.7 1.6 fusion.44
  130.7 1.3 fusion.46
  131.9 1.0 fusion.43
  132.9 1.6 fusion.44
  134.9 1.3 fusion.46
  136.1 1.0 fusion.43
  137.2 1.6 fusion.44
  139.1 1.3 fusion.46
  140.4 1.0 fusion.43
  141.4 1.6 fusion.44
  143.3 1.3 fusion.46
  144.6 1.0 fusion.43
  145.6 1.6 fusion.44
  147.5 1.3 fusion.46
  148.8 1.0 fusion.43
  149.8 1.6 fusion.44
  151.7 1.3 fusion.46
  153.0 1.0 fusion.43
  154.0 1.6 fusion.44
  155.9 1.3 fusion.46
  157.2 2.3 %copy.31 = bf16[256,2048]{1,0:T(8,128)(2,1)} copy(bf16[256,2048]{0,1:T(8,128)(2,1)} %bitcast.9) | data formatting | bytes 2097152 | tf_op jit(solution)/shard_map/reshape | solution.py:48
  (38 shorter events, 6.5 us)
Async XLA Ops:
  0.0 32.8 %copy-start = (bf16[256,1024]{1,0:T(8,128)(2,1)S(1)}, bf16[256,1024]{1,0:T(8,128)(2,1)}, u32[]{:S(2)}) copy-start(bf16[256,1024]{1,0:T(8,128)(2,1)} %param.8) | copy-start | bytes 1572868
  6.0 18.6 %collective-permute-start.4 = (s32[256]{0:T(256)S(1)}, s32[256]{0:T(256)S(1)}, u32[]{:S(2)}, u32[]{:S(2)}) collective-permute-start(s32[256]{0:T(256)S(1)} %broadcast_add_fusion.1), channel_id=1, source_target_pairs={{0,8},{2,10},{4,12},{6,14},{8,16},{10,18},{12,20},{14,22},{16,24},... | collective-permute-start | bytes 3080 | tf_op jit(solution)/shard_map/ppermute | solution.py:16
  9.5 18.1 %collective-permute-start.5 = (s32[256]{0:T(256)S(1)}, s32[256]{0:T(256)S(1)}, u32[]{:S(2)}, u32[]{:S(2)}) collective-permute-start(s32[256]{0:T(256)S(1)} %broadcast_add_fusion.1), channel_id=1, source_target_pairs={{0,6},{2,8},{4,10},{6,12},{8,14},{10,16},{12,18},{14,20},{16,22},{... | collective-permute-start | bytes 3080 | tf_op jit(solution)/shard_map/ppermute | solution.py:16
  11.4 19.1 %collective-permute-start.6 = (s32[256]{0:T(256)S(1)}, s32[256]{0:T(256)S(1)}, u32[]{:S(2)}, u32[]{:S(2)}) collective-permute-start(s32[256]{0:T(256)S(1)} %broadcast_add_fusion.1), channel_id=1, source_target_pairs={{0,4},{2,6},{4,8},{6,10},{8,12},{10,14},{12,16},{14,18},{16,20},{1... | collective-permute-start | bytes 3080 | tf_op jit(solution)/shard_map/ppermute | solution.py:16
  14.5 18.2 %collective-permute-start.7 = (s32[256]{0:T(256)S(1)}, s32[256]{0:T(256)S(1)}, u32[]{:S(2)}, u32[]{:S(2)}) collective-permute-start(s32[256]{0:T(256)S(1)} %broadcast_add_fusion.1), channel_id=1, source_target_pairs={{0,2},{2,4},{4,6},{6,8},{8,10},{10,12},{12,14},{14,16},{16,18},{18... | collective-permute-start | bytes 3080 | tf_op jit(solution)/shard_map/ppermute | solution.py:16
  19.1 38.0 %collective-permute-start.8 = (bf16[256,1024]{0,1:T(8,128)(2,1)S(1)}, bf16[256,1024]{0,1:T(8,128)(2,1)S(1)}, u32[]{:S(2)}, u32[]{:S(2)}) collective-permute-start(bf16[256,1024]{0,1:T(8,128)(2,1)S(1)} %copy.21), channel_id=1, source_target_pairs={{0,8},{2,10},{4,12},{6,14},{8,16},{10,18},{12,20},{14,22},{16,24},... | collective-permute-start | bytes 1572872 | tf_op jit(solution)/shard_map/ppermute | solution.py:16
  24.6 34.4 %collective-permute-start.9 = (bf16[256,1024]{0,1:T(8,128)(2,1)S(1)}, bf16[256,1024]{0,1:T(8,128)(2,1)S(1)}, u32[]{:S(2)}, u32[]{:S(2)}) collective-permute-start(bf16[256,1024]{0,1:T(8,128)(2,1)S(1)} %copy.21), channel_id=1, source_target_pairs={{0,6},{2,8},{4,10},{6,12},{8,14},{10,16},{12,18},{14,20},{16,22},{... | collective-permute-start | bytes 1572872 | tf_op jit(solution)/shard_map/ppermute | solution.py:16
  27.6 50.2 %collective-permute-start.10 = (bf16[256,1024]{0,1:T(8,128)(2,1)S(1)}, bf16[256,1024]{0,1:T(8,128)(2,1)S(1)}, u32[]{:S(2)}, u32[]{:S(2)}) collective-permute-start(bf16[256,1024]{0,1:T(8,128)(2,1)S(1)} %copy.21), channel_id=1, source_target_pairs={{0,4},{2,6},{4,8},{6,10},{8,12},{10,14},{12,16},{14,18},{16,20},{1... | collective-permute-start | bytes 1572872 | tf_op jit(solution)/shard_map/ppermute | solution.py:16
  30.5 53.9 %collective-permute-start.11 = (bf16[256,1024]{0,1:T(8,128)(2,1)S(1)}, bf16[256,1024]{0,1:T(8,128)(2,1)S(1)}, u32[]{:S(2)}, u32[]{:S(2)}) collective-permute-start(bf16[256,1024]{0,1:T(8,128)(2,1)S(1)} %copy.21), channel_id=1, source_target_pairs={{0,2},{2,4},{4,6},{6,8},{8,10},{10,12},{12,14},{14,16},{16,18},{18... | collective-permute-start | bytes 1572872 | tf_op jit(solution)/shard_map/ppermute | solution.py:16
  32.8 51.7 %collective-permute-start = (bf16[256,1024]{1,0:T(8,128)(2,1)S(1)}, bf16[256,1024]{1,0:T(8,128)(2,1)S(1)}, u32[]{:S(2)}, u32[]{:S(2)}) collective-permute-start(bf16[256,1024]{1,0:T(8,128)(2,1)S(1)} %copy-done), channel_id=1, source_target_pairs={{0,8},{2,10},{4,12},{6,14},{8,16},{10,18},{12,20},{14,22},{16,24},... | collective-permute-start | bytes 1572872 | tf_op jit(solution)/shard_map/ppermute | solution.py:16
  57.1 28.3 %collective-permute-start.1 = (bf16[256,1024]{1,0:T(8,128)(2,1)S(1)}, bf16[256,1024]{1,0:T(8,128)(2,1)S(1)}, u32[]{:S(2)}, u32[]{:S(2)}) collective-permute-start(bf16[256,1024]{1,0:T(8,128)(2,1)S(1)} %copy-done), channel_id=1, source_target_pairs={{0,6},{2,8},{4,10},{6,12},{8,14},{10,16},{12,18},{14,20},{16,22},{... | collective-permute-start | bytes 1572872 | tf_op jit(solution)/shard_map/ppermute | solution.py:16
  59.0 49.3 %collective-permute-start.2 = (bf16[256,1024]{1,0:T(8,128)(2,1)S(1)}, bf16[256,1024]{1,0:T(8,128)(2,1)S(1)}, u32[]{:S(2)}, u32[]{:S(2)}) collective-permute-start(bf16[256,1024]{1,0:T(8,128)(2,1)S(1)} %copy-done), channel_id=1, source_target_pairs={{0,4},{2,6},{4,8},{6,10},{8,12},{10,14},{12,16},{14,18},{16,20},{1... | collective-permute-start | bytes 1572872 | tf_op jit(solution)/shard_map/ppermute | solution.py:16
  77.8 41.0 %collective-permute-start.3 = (bf16[256,1024]{1,0:T(8,128)(2,1)S(1)}, bf16[256,1024]{1,0:T(8,128)(2,1)S(1)}, u32[]{:S(2)}, u32[]{:S(2)}) collective-permute-start(bf16[256,1024]{1,0:T(8,128)(2,1)S(1)} %copy-done), channel_id=1, source_target_pairs={{0,2},{2,4},{4,6},{6,8},{8,10},{10,12},{12,14},{14,16},{16,18},{18... | collective-permute-start | bytes 1572872 | tf_op jit(solution)/shard_map/ppermute | solution.py:16
  84.4 35.2 %copy-start.1 = (bf16[1280,1024]{0,1:T(8,128)(2,1)}, bf16[1280,1024]{0,1:T(8,128)(2,1)S(1)}, u32[]{:S(2)}) copy-start(bf16[1280,1024]{0,1:T(8,128)(2,1)S(1)} %constant_dynamic-update-slice_fusion.5) | copy-start | bytes 7864324
where the time goes:
time: 160 us; the launch traced here: 159 us
  waiting for transfers between devices  71.1 us (44%)
  starting transfers between devices  35.1 us (22%)
  matrix products  22.6 us (14%)
  local copies, waits for them, and re-layouts  13.2 us (8%)
  other arithmetic  11 us (7%)
  blocking collectives  6 us (4%)
    ppermute x12, waiting for transfers between devices, from_behind(): lax.ppermute(value, axis, [(source, source + steps) for source in range(i...  71.1 us
    ppermute x12, starting transfers between devices, from_behind(): lax.ppermute(value, axis, [(source, source + steps) for source in range(i...  35.1 us
    dot_general x8, matrix products, one_head(): jnp.einsum('tgd,sd->gts', head_q, head_k, preferred_element_type=jnp.floa...  12.4 us
    dot_general x8, matrix products, one_head(): jnp.einsum('gts,sd->tgd', rounded, head_v, preferred_element_type=jnp.flo...  10.1 us
    and x8, other arithmetic, attend(): (key_ids[None, :] == query_ids[:, None]) & (key_pos[None, :] <= query_pos...  8.07 us
    unnamed x18, local copies, waits for them, and re-layouts  7.11 us
    all_gather x1, blocking collectives, body(): own_ids = lax.all_gather(segment_ids, 'head', axis=0, tiled=True)  6 us
    concatenate x2, local copies, waits for them, and re-layouts, body(): all_values = jnp.concatenate([piece[1] for piece in ordered], axis=0)  3.81 us
  transfers between devices with their start and end apart: 12, of which 5 were waited for; matrix products, arithmetic and copies ran while one was open for 4% of the time, Pallas kernels for 0%

commit v1 on v0

v1 whole, which is shorter than its diff:
```python
import functools

import jax
import jax.numpy as jnp
from jax import lax
from jax.experimental import pallas as pl
from jax.experimental.pallas import tpu as pltpu
from jax.sharding import PartitionSpec as P

HEAD_WIDTH = 128
WINDOW = 1024
SCALE = 168.0 ** (-0.5)
LOG2E = 1.4426950408889634
MESH = pl.DeviceIdType.MESH


def kernel(n_seq, q_hbm, k_hbm, v_hbm, id_hbm, out_hbm,
           kv, qbuf, obuf, ids, bias, p_buf, l_buf,
           ld_sem, q_sem, o_sem, id_sem, id_send, id_recv,
           y_send, y_recv, x_send, x_recv, a_send, b_send, c1_recv, c3_recv):
    rows = k_hbm.shape[0]
    heads = k_hbm.shape[1] // HEAD_WIDTH
    half = id_hbm.shape[1]
    span = kv.shape[2]
    s = lax.axis_index("seq")
    head = lax.axis_index("head")
    core = lax.rem(s, 2)
    chip = lax.rem(s // 2, 2)
    y_next = (lax.rem(s + 4, n_seq), head)
    y_prev = (lax.rem(s + n_seq - 4, n_seq), head)
    x_peer = (s + 2 - 4 * chip, head)
    c_peer = (s + 1 - 2 * core, head)
    h_peer = (s, 1 - head)

    x_src = 4 * (1 - chip)
    a_src, a_dst = 4 * (1 - core), 3 - 2 * core
    b_dst = 1 + 2 * core

    def part(c, h, slot):
        return kv.at[c, h, pl.ds(pl.multiple_of(slot * rows, rows), rows), :]

    def load(c, h, ref):
        return pltpu.make_async_copy(
            ref.at[:, pl.ds(pl.multiple_of(h * HEAD_WIDTH, HEAD_WIDTH), HEAD_WIDTH)],
            part(c, h, 4), ld_sem.at[c, h])

    def load_q(h):
        return pltpu.make_async_copy(
            q_hbm.at[:, pl.ds(pl.multiple_of(h * 256, 256), 256)], qbuf.at[h], q_sem.at[h])

    def store(h):
        return pltpu.make_async_copy(
            obuf.at[h], out_hbm.at[:, pl.ds(pl.multiple_of(h * 256, 256), 256)], o_sem.at[h])

    def remote(src, dst, send, recv, dev):
        return pltpu.make_async_remote_copy(
            src_ref=src, dst_ref=dst, send_sem=send, recv_sem=recv,
            device_id=dev, device_id_type=MESH)

    def y_copy(c, h):
        return remote(part(c, h, 4), part(c, h, 0), y_send.at[c, h], y_recv.at[c, h], y_next)

    def x_copy(c, h):
        return remote(part(c, h, x_src), part(c, h, 2), x_send.at[c, h], x_recv.at[c, h], x_peer)

    def a_copy(c, h):
        return remote(part(c, h, a_src), part(c, h, a_dst), a_send.at[c, h],
                      c1_recv.at[c, h], c_peer)

    def b_copy(c, h):
        return remote(part(c, h, 2), part(c, h, b_dst), b_send.at[c, h],
                      c3_recv.at[c, h], c_peer)

    own_id = pltpu.make_async_copy(id_hbm, ids.at[head, 4], id_sem)
    own_id.start()

    @pl.loop(0, heads)
    def _(h):
        load(0, h, k_hbm).start()
        load(1, h, v_hbm).start()

    @pl.loop(0, heads)
    def _(h):
        load_q(h).start()

    barrier = pltpu.get_barrier_semaphore()
    for peer in (y_next, y_prev, x_peer, c_peer, h_peer):
        pl.semaphore_signal(barrier, inc=1, device_id=peer, device_id_type=MESH)
    own_id.wait()
    pl.semaphore_wait(barrier, 5)

    id_y = remote(ids.at[head, 4], ids.at[head, 0], id_send.at[0], id_recv.at[0], y_next)
    id_y.start()

    @pl.loop(0, heads)
    def _(h):
        load(0, h, k_hbm).wait()
        y_copy(0, h).start()
        load(1, h, v_hbm).wait()
        y_copy(1, h).start()

    id_x = remote(ids.at[head, x_src], ids.at[head, 2], id_send.at[1], id_recv.at[1], x_peer)
    id_a = remote(ids.at[head, a_src], ids.at[head, a_dst], id_send.at[2], id_recv.at[2], c_peer)
    id_b = remote(ids.at[head, 2], ids.at[head, b_dst], id_send.at[3], id_recv.at[3], c_peer)
    id_h = remote(ids.at[head], ids.at[head], id_send.at[4], id_recv.at[4], h_peer)
    id_y.wait_recv()
    id_x.start()
    id_a.start()
    id_x.wait_recv()
    id_b.start()
    id_a.wait_recv()
    id_b.wait_recv()
    id_h.start()

    def relay_y(c, h):
        y_copy(c, h).wait_recv()
        x_copy(c, h).start()
        a_copy(c, h).start()

    def relay_x(c, h):
        x_copy(c, h).wait_recv()
        b_copy(c, h).start()

    def arrive(c, h):
        remote(part(c, h, 4), part(c, h, 1), a_send.at[c, h], c1_recv.at[c, h], c_peer).wait_recv()
        remote(part(c, h, 4), part(c, h, 1), a_send.at[c, h], c3_recv.at[c, h], c_peer).wait_recv()

    def make_bias():
        own = [
            jnp.swapaxes(jnp.broadcast_to(ids[t, 4], (half, half)), 0, 1)
            for t in range(2)
        ]
        row = lax.broadcasted_iota(jnp.int32, (half, half), 0)
        lane = lax.broadcasted_iota(jnp.int32, (half, half), 1)
        for top in range(2):
            for slot in range(5):
                for t in range(2):
                    key_pos = slot * rows + t * half - 4 * rows
                    gap = row + (top * half - key_pos) - lane
                    visible = (
                        (own[top] == ids[t, slot])
                        & (gap >= 0) & (gap < WINDOW)
                        & (lane + (s * rows + key_pos) >= 0)
                    )
                    bias[pl.ds(top * half, half), pl.ds(slot * rows + t * half, half)] = (
                        jnp.where(visible, 0.0, -1e30)
                    )

    def weigh(h):
        load_q(h).wait()
        for t in range(2):
            scores = lax.dot_general(
                qbuf[h, :, pl.ds(t * HEAD_WIDTH, HEAD_WIDTH)], kv[0, h],
                (((1,), (1,)), ((), ())), preferred_element_type=jnp.float32)
            scores = scores * (SCALE * LOG2E) + bias[...]
            top = jnp.max(scores, axis=1, keepdims=True)
            weights = jnp.exp2(scores - top)
            l_buf[t] = jnp.broadcast_to(jnp.sum(weights, axis=1, keepdims=True), (rows, HEAD_WIDTH))
            p_buf[t] = weights.astype(jnp.bfloat16)

    def mix(h):
        for t in range(2):
            mixed = jnp.dot(p_buf[t], kv[1, h], preferred_element_type=jnp.float32)
            obuf[h, :, pl.ds(t * HEAD_WIDTH, HEAD_WIDTH)] = (mixed / l_buf[t]).astype(jnp.bfloat16)
        store(h).start()

    @pl.loop(0, heads + 1)
    def _(h):
        @pl.when(h < heads)
        def _():
            relay_y(0, h)

        @pl.when(h >= 1)
        def _():
            relay_x(1, h - 1)
            arrive(0, h - 1)

            @pl.when(h == 1)
            def _():
                id_h.wait_recv()
                make_bias()

            weigh(h - 1)

        @pl.when(h < heads)
        def _():
            relay_y(1, h)
            relay_x(0, h)

        @pl.when(h >= 1)
        def _():
            arrive(1, h - 1)
            mix(h - 1)

    for copy in (id_y, id_x, id_a, id_b, id_h):
        copy.wait_send()

    @pl.loop(0, heads)
    def _(h):
        for c in range(2):
            y_copy(c, h).wait_send()
            x_copy(c, h).wait_send()
            a_copy(c, h).wait_send()
            b_copy(c, h).wait_send()
        store(h).wait()


def body(queries, keys, values, segment_ids):
    rows, width = keys.shape
    heads = width // HEAD_WIDTH
    n_seq = lax.axis_size("seq")
    half = segment_ids.shape[0]
    dma = pltpu.SemaphoreType.DMA
    return pl.pallas_call(
        functools.partial(kernel, n_seq),
        out_shape=jax.ShapeDtypeStruct(queries.shape, queries.dtype),
        in_specs=[pl.BlockSpec(memory_space=pl.ANY)] * 4,
        out_specs=pl.BlockSpec(memory_space=pl.ANY),
        scratch_shapes=[
            pltpu.VMEM((2, heads, 5 * rows, HEAD_WIDTH), jnp.bfloat16),
            pltpu.VMEM((heads, rows, 256), jnp.bfloat16),
            pltpu.VMEM((heads, rows, 256), jnp.bfloat16),
            pltpu.VMEM((2, 5, 1, half), jnp.int32),
            pltpu.VMEM((rows, 5 * rows), jnp.float32),
            pltpu.VMEM((2, rows, 5 * rows), jnp.bfloat16),
            pltpu.VMEM((2, rows, HEAD_WIDTH), jnp.float32),
            dma((2, heads)), dma((heads,)), dma((heads,)), dma, dma((5,)), dma((5,)),
            dma((2, heads)), dma((2, heads)), dma((2, heads)), dma((2, heads)),
            dma((2, heads)), dma((2, heads)), dma((2, heads)), dma((2, heads)),
        ],
        compiler_params=pltpu.CompilerParams(collective_id=0, has_side_effects=True),
    )(queries, keys, values, segment_ids.reshape(1, half))


def solution(mesh):
    in_specs = (P("seq", "head"), P("seq", "head"), P("seq", "head"), P(("seq", "head")))
    out_specs = P("seq", "head")
    return jax.shard_map(body, mesh=mesh, in_specs=in_specs, out_specs=out_specs, check_vma=False)
```

time: 160 us -> 60.8 us (0.38)
  the two profiles are of different devices: /device:TPU:132 before, /device:TPU:3 now
where the time goes in v1:
time: 60.8 us; the launch traced here: 60.7 us
  Pallas kernels  58.4 us (96%)
  local copies, waits for them, and re-layouts  2.3 us (4%)
    pallas_call x1, Pallas kernels, body(): pl.pallas_call(functools.partial(kernel, n_seq), out_shape=jax.ShapeDtype...  58.4 us
    unnamed x1, local copies, waits for them, and re-layouts  2.3 us

profile of v1, /device:TPU:3, one launch (start us, length us, event | category | flops | bytes accessed | tf_op | source)
XLA Modules:
  0.0 60.7 jit_solution(13659715521606713190)
XLA Ops:
  0.0 58.4 %shard_map.46 = bf16[256,2048]{1,0:T(8,128)(2,1)} custom-call(bf16[256,2048]{1,0:T(8,128)(2,1)} %q_hbm.1, bf16[256,1024]{1,0:T(8,128)(2,1)} %k_hbm.1, bf16[256,1024]{1,0:T(8,128)(2,1)} %v_hbm.1, s32[1,128]{1,0:T(1,128)} %bitcast.1), custom_call_target="tpu_custom_call" | custom-call | tf_op jit(solution)/shard_map/pallas_call | solution.py:214
  58.4 2.3 %copy.6 = bf16[256,2048]{1,0:T(8,128)(2,1)} copy(bf16[256,2048]{1,0:T(8,128)(2,1)} %shard_map.46) | data formatting | bytes 2097152

commit v2 on v1

--- a/solution.py
+++ b/solution.py
@@ -12,11 +12,12 @@
 SCALE = 168.0 ** (-0.5)
 LOG2E = 1.4426950408889634
 MESH = pl.DeviceIdType.MESH
-
-
-def kernel(n_seq, q_hbm, k_hbm, v_hbm, id_hbm, out_hbm,
-           kv, qbuf, obuf, ids, bias, p_buf, l_buf,
-           ld_sem, q_sem, o_sem, id_sem, id_send, id_recv,
+X_LAG = 3
+
+
+def kernel(n_seq, q_hbm, k_hbm, v_hbm, id_hbm, out,
+           kv, qbuf, ids, bias, p_buf, l_buf,
+           ld_sem, q_sem, id_sem, id_send, id_recv,
            y_send, y_recv, x_send, x_recv, a_send, b_send, c1_recv, c3_recv):
     rows = k_hbm.shape[0]
     heads = k_hbm.shape[1] // HEAD_WIDTH
@@ -48,10 +49,6 @@
         return pltpu.make_async_copy(
             q_hbm.at[:, pl.ds(pl.multiple_of(h * 256, 256), 256)], qbuf.at[h], q_sem.at[h])
 
-    def store(h):
-        return pltpu.make_async_copy(
-            obuf.at[h], out_hbm.at[:, pl.ds(pl.multiple_of(h * 256, 256), 256)], o_sem.at[h])
-
     def remote(src, dst, send, recv, dev):
         return pltpu.make_async_remote_copy(
             src_ref=src, dst_ref=dst, send_sem=send, recv_sem=recv,
@@ -71,6 +68,18 @@
         return remote(part(c, h, 2), part(c, h, b_dst), b_send.at[c, h],
                       c3_recv.at[c, h], c_peer)
 
+    first = s < 4
+    last = s >= n_seq - 4
+    steps = 2 * heads
+
+    def split(i):
+        return lax.rem(i, 2), i // 2
+
+    def fill(c, h, ref):
+        return pltpu.make_async_copy(
+            ref.at[:, pl.ds(pl.multiple_of(h * HEAD_WIDTH, HEAD_WIDTH), HEAD_WIDTH)],
+            part(c, h, 0), y_recv.at[c, h])
+
     own_id = pltpu.make_async_copy(id_hbm, ids.at[head, 4], id_sem)
     own_id.start()
 
@@ -79,51 +88,72 @@
         load(0, h, k_hbm).start()
         load(1, h, v_hbm).start()
 
+    barrier = pltpu.get_barrier_semaphore()
+    for peer in (x_peer, c_peer, h_peer):
+        pl.semaphore_signal(barrier, inc=1, device_id=peer, device_id_type=MESH)
+
+    @pl.when(jnp.logical_not(first))
+    def _():
+        pl.semaphore_signal(barrier, inc=1, device_id=y_prev, device_id_type=MESH)
+
+    @pl.when(jnp.logical_not(last))
+    def _():
+        pl.semaphore_signal(barrier, inc=1, device_id=y_next, device_id_type=MESH)
+
     @pl.loop(0, heads)
     def _(h):
         load_q(h).start()
 
-    barrier = pltpu.get_barrier_semaphore()
-    for peer in (y_next, y_prev, x_peer, c_peer, h_peer):
-        pl.semaphore_signal(barrier, inc=1, device_id=peer, device_id_type=MESH)
+    @pl.when(first)
+    def _():
+        pltpu.make_async_copy(id_hbm, ids.at[head, 0], id_recv.at[0]).start()
+
+        @pl.loop(0, heads)
+        def _(h):
+            fill(0, h, k_hbm).start()
+            fill(1, h, v_hbm).start()
+
     own_id.wait()
-    pl.semaphore_wait(barrier, 5)
+    pl.semaphore_wait(barrier, 5 - first.astype(jnp.int32) - last.astype(jnp.int32))
 
     id_y = remote(ids.at[head, 4], ids.at[head, 0], id_send.at[0], id_recv.at[0], y_next)
-    id_y.start()
-
-    @pl.loop(0, heads)
-    def _(h):
-        load(0, h, k_hbm).wait()
-        y_copy(0, h).start()
-        load(1, h, v_hbm).wait()
-        y_copy(1, h).start()
-
     id_x = remote(ids.at[head, x_src], ids.at[head, 2], id_send.at[1], id_recv.at[1], x_peer)
     id_a = remote(ids.at[head, a_src], ids.at[head, a_dst], id_send.at[2], id_recv.at[2], c_peer)
     id_b = remote(ids.at[head, 2], ids.at[head, b_dst], id_send.at[3], id_recv.at[3], c_peer)
     id_h = remote(ids.at[head], ids.at[head], id_send.at[4], id_recv.at[4], h_peer)
+
+    @pl.when(jnp.logical_not(last))
+    def _():
+        id_y.start()
+
+    @pl.loop(0, heads)
+    def _(h):
+        load(0, h, k_hbm).wait()
+        load(1, h, v_hbm).wait()
+
+        @pl.when(jnp.logical_not(last))
+        def _():
+            y_copy(0, h).start()
+            y_copy(1, h).start()
+
     id_y.wait_recv()
     id_x.start()
     id_a.start()
-    id_x.wait_recv()
-    id_b.start()
-    id_a.wait_recv()
-    id_b.wait_recv()
-    id_h.start()
-
-    def relay_y(c, h):
+
+    def relay_y(i):
+        c, h = split(i)
         y_copy(c, h).wait_recv()
         x_copy(c, h).start()
         a_copy(c, h).start()
 
-    def relay_x(c, h):
+    def relay_x(i):
+        c, h = split(i)
         x_copy(c, h).wait_recv()
         b_copy(c, h).start()
 
     def arrive(c, h):
-        remote(part(c, h, 4), part(c, h, 1), a_send.at[c, h], c1_recv.at[c, h], c_peer).wait_recv()
-        remote(part(c, h, 4), part(c, h, 1), a_send.at[c, h], c3_recv.at[c, h], c_peer).wait_recv()
+        a_copy(c, h).wait_recv()
+        b_copy(c, h).wait_recv()
 
     def make_bias():
         own = [
@@ -161,48 +191,61 @@
     def mix(h):
         for t in range(2):
             mixed = jnp.dot(p_buf[t], kv[1, h], preferred_element_type=jnp.float32)
-            obuf[h, :, pl.ds(t * HEAD_WIDTH, HEAD_WIDTH)] = (mixed / l_buf[t]).astype(jnp.bfloat16)
-        store(h).start()
-
-    @pl.loop(0, heads + 1)
-    def _(h):
-        @pl.when(h < heads)
-        def _():
-            relay_y(0, h)
-
-        @pl.when(h >= 1)
-        def _():
-            relay_x(1, h - 1)
-            arrive(0, h - 1)
-
-            @pl.when(h == 1)
+            out[:, pl.ds(pl.multiple_of(h * 256 + t * HEAD_WIDTH, HEAD_WIDTH), HEAD_WIDTH)] = (
+                mixed / l_buf[t]).astype(jnp.bfloat16)
+
+    relay_y(0)
+    relay_y(1)
+    id_x.wait_recv()
+    id_b.start()
+    id_a.wait_recv()
+    id_b.wait_recv()
+    id_h.start()
+
+    @pl.loop(1, heads + 2)
+    def _(h):
+        for c in range(2):
+            i = 2 * h + c
+
+            @pl.when(i < steps)
             def _():
-                id_h.wait_recv()
-                make_bias()
-
-            weigh(h - 1)
-
-        @pl.when(h < heads)
-        def _():
-            relay_y(1, h)
-            relay_x(0, h)
-
-        @pl.when(h >= 1)
-        def _():
-            arrive(1, h - 1)
-            mix(h - 1)
-
-    for copy in (id_y, id_x, id_a, id_b, id_h):
+                relay_y(i)
+
+            @pl.when((i >= X_LAG) & (i < steps + X_LAG))
+            def _():
+                relay_x(i - X_LAG)
+
+            @pl.when(h >= 2)
+            def _():
+                arrive(c, h - 2)
+                if c == 0:
+                    @pl.when(h == 2)
+                    def _():
+                        id_h.wait_recv()
+                        make_bias()
+
+                    weigh(h - 2)
+                else:
+                    mix(h - 2)
+
+    for copy in (id_x, id_a, id_b, id_h):
         copy.wait_send()
 
+    @pl.when(jnp.logical_not(last))
+    def _():
+        id_y.wait_send()
+
+        @pl.loop(0, heads)
+        def _(h):
+            y_copy(0, h).wait_send()
+            y_copy(1, h).wait_send()
+
     @pl.loop(0, heads)
     def _(h):
         for c in range(2):
-            y_copy(c, h).wait_send()
             x_copy(c, h).wait_send()
             a_copy(c, h).wait_send()
             b_copy(c, h).wait_send()
-        store(h).wait()
 
 
 def body(queries, keys, values, segment_ids):
@@ -213,18 +256,17 @@
     dma = pltpu.SemaphoreType.DMA
     return pl.pallas_call(
         functools.partial(kernel, n_seq),
-        out_shape=jax.ShapeDtypeStruct(queries.shape, queries.dtype),
+        out_shape=pltpu.VMEM(queries.shape, queries.dtype),
         in_specs=[pl.BlockSpec(memory_space=pl.ANY)] * 4,
-        out_specs=pl.BlockSpec(memory_space=pl.ANY),
+        out_specs=pl.BlockSpec(memory_space=pltpu.VMEM),
         scratch_shapes=[
             pltpu.VMEM((2, heads, 5 * rows, HEAD_WIDTH), jnp.bfloat16),
-            pltpu.VMEM((heads, rows, 256), jnp.bfloat16),
             pltpu.VMEM((heads, rows, 256), jnp.bfloat16),
             pltpu.VMEM((2, 5, 1, half), jnp.int32),
             pltpu.VMEM((rows, 5 * rows), jnp.float32),
             pltpu.VMEM((2, rows, 5 * rows), jnp.bfloat16),
             pltpu.VMEM((2, rows, HEAD_WIDTH), jnp.float32),
-            dma((2, heads)), dma((heads,)), dma((heads,)), dma, dma((5,)), dma((5,)),
+            dma((2, heads)), dma((heads,)), dma, dma((5,)), dma((5,)),
             dma((2, heads)), dma((2, heads)), dma((2, heads)), dma((2, heads)),
             dma((2, heads)), dma((2, heads)), dma((2, heads)), dma((2, heads)),
         ],

time: 60.8 us -> 38.1 us (0.63)
  the two profiles are of different devices: /device:TPU:3 before, /device:TPU:192 now
where the time goes in v2:
time: 38.1 us; the launch traced here: 37.6 us
  Pallas kernels  36.6 us (96%)
  local copies, waits for them, and re-layouts  0.97 us (3%)
    pallas_call x1, Pallas kernels, body(): pl.pallas_call(functools.partial(kernel, n_seq), out_shape=pltpu.VMEM(que...  36.6 us
    unnamed x1, local copies, waits for them, and re-layouts  0.97 us

profile of v2, /device:TPU:192, one launch (start us, length us, event | category | flops | bytes accessed | tf_op | source)
XLA Modules:
  0.0 37.6 jit_solution(18066471775873956019)
XLA Ops:
  0.0 36.6 %shard_map.46 = bf16[256,2048]{1,0:T(8,128)(2,1)S(1)} custom-call(bf16[256,2048]{1,0:T(8,128)(2,1)} %q_hbm.1, bf16[256,1024]{1,0:T(8,128)(2,1)} %k_hbm.1, bf16[256,1024]{1,0:T(8,128)(2,1)} %v_hbm.1, s32[1,128]{1,0:T(1,128)} %bitcast.1), custom_call_target="tpu_custom_call" | custom-call | tf_op jit(solution)/shard_map/pallas_call | solution.py:257
  36.6 1.0 %copy.6 = bf16[256,2048]{1,0:T(8,128)(2,1)} copy(bf16[256,2048]{1,0:T(8,128)(2,1)S(1)} %shard_map.46) | data formatting | bytes 2097152

commit v3 on v2

v3 whole, which is shorter than its diff:
```python
import functools

import jax
import jax.numpy as jnp
from jax import lax
from jax.experimental import pallas as pl
from jax.experimental.pallas import tpu as pltpu
from jax.sharding import PartitionSpec as P

HEAD_WIDTH = 128
WINDOW = 1024
SCALE = 168.0 ** (-0.5)
LOG2E = 1.4426950408889634
MESH = pl.DeviceIdType.MESH
X_LAG = 2
UNIT_LAG = 4
EARLY = 14
HELD = 13
AHEAD = 4


def kernel(n_seq, q_hbm, k_hbm, v_hbm, id_hbm, out,
           kv, early, qbuf, ids, bias, p_buf, l_buf,
           ld_sem, q_sem, id_sem, e_sem, id_send, id_recv,
           y_send, y_recv, x_send, x_recv, a_send, a_recv, b_send, b_recv):
    rows = k_hbm.shape[0]
    heads = k_hbm.shape[1] // HEAD_WIDTH
    half = id_hbm.shape[1]
    span = kv.shape[2]
    s = lax.axis_index("seq")
    head = lax.axis_index("head")
    core = lax.rem(s, 2)
    chip = lax.rem(s // 2, 2)
    y_next = (lax.rem(s + 4, n_seq), head)
    y_prev = (lax.rem(s + n_seq - 4, n_seq), head)
    x_peer = (s + 2 - 4 * chip, head)
    c_peer = (s + 1 - 2 * core, head)
    cross = (s + 2 - 4 * chip, 1 - head)

    x_src = 4 * (1 - chip)
    a_src, a_dst = 4 * (1 - core), 3 - 2 * core
    b_dst = 1 + 2 * core

    steps = 2 * heads

    def unit(i):
        c = 1 - lax.rem(i, 2) + i // (steps - 1) - (steps - 1 - i) // (steps - 1)
        return c, (i + 1) // 2 - c

    def chunk(i, slot):
        c, h = unit(i)
        return kv.at[c, h, pl.ds(pl.multiple_of(slot * rows, rows), rows), :]

    def columns(ref, h):
        return ref.at[:, pl.ds(pl.multiple_of(h * HEAD_WIDTH, HEAD_WIDTH), HEAD_WIDTH)]

    def own(i, slot, sem):
        return pltpu.make_async_copy(columns(k_hbm, 0), chunk(i, slot), sem.at[i])

    def start_own(i, slot, sem):
        c, h = unit(i)

        @pl.when(c == 0)
        def _():
            pltpu.make_async_copy(columns(k_hbm, h), chunk(i, slot), sem.at[i]).start()

        @pl.when(c == 1)
        def _():
            pltpu.make_async_copy(columns(v_hbm, h), chunk(i, slot), sem.at[i]).start()

    def load_q(h):
        return pltpu.make_async_copy(
            q_hbm.at[:, pl.ds(pl.multiple_of(h * 256, 256), 256)], qbuf.at[h], q_sem.at[h])

    def remote(src, dst, send, recv, dev):
        return pltpu.make_async_remote_copy(
            src_ref=src, dst_ref=dst, send_sem=send, recv_sem=recv,
            device_id=dev, device_id_type=MESH)

    def y_copy(i):
        return remote(chunk(i, 4), chunk(i, 0), y_send, y_recv.at[i], y_next)

    def x_copy(i, send=x_send):
        return remote(chunk(i, x_src), chunk(i, 2), send, x_recv.at[i], x_peer)

    def a_copy(i):
        return remote(chunk(i, a_src), chunk(i, a_dst), a_send, a_recv.at[i], c_peer)

    def b_copy(i):
        return remote(chunk(i, 2), chunk(i, b_dst), b_send, b_recv.at[i], c_peer)

    def early_x():
        return remote(chunk(EARLY, 4), early, x_send, e_sem.at[0], x_peer)

    def early_y():
        return remote(early, chunk(EARLY, 2), e_sem.at[1], x_recv.at[EARLY], y_next)

    first = s < 4
    last = s >= n_seq - 4
    def x_sends(i):
        return (i < steps) & ((chip == 0) | (i != EARLY))

    barrier = pltpu.get_barrier_semaphore()

    @pl.when(jnp.logical_not(first))
    def _():
        pl.semaphore_signal(barrier, inc=1, device_id=y_prev, device_id_type=MESH)

    @pl.when(jnp.logical_not(last))
    def _():
        pl.semaphore_signal(barrier, inc=1, device_id=y_next, device_id_type=MESH)

    for peer in (cross, x_peer, c_peer):
        pl.semaphore_signal(barrier, inc=1, device_id=peer, device_id_type=MESH)

    own_id = pltpu.make_async_copy(id_hbm, ids.at[head, core, chip, 1], id_sem)
    own_id.start()

    @pl.loop(0, steps)
    def _(i):
        start_own(i, 4, ld_sem)

    @pl.loop(0, heads)
    def _(h):
        load_q(h).start()

    @pl.when(first)
    def _():
        pltpu.make_async_copy(id_hbm, ids.at[head, core, chip, 0], id_recv.at[0]).start()

        @pl.loop(0, steps)
        def _(i):
            start_own(i, 0, y_recv)

    own_id.wait()
    pl.semaphore_wait(barrier, 5 - first.astype(jnp.int32) - last.astype(jnp.int32))

    def id_copy(n, src, dst, dev):
        return remote(src, dst, id_send.at[n], id_recv.at[n], dev)

    mine = ids.at[head, core, chip]
    id_y = id_copy(0, mine.at[1], mine.at[0], y_next)
    id_x = id_copy(1, mine, mine, x_peer)
    id_c = id_copy(2, ids.at[head, core], ids.at[head, core], c_peer)
    id_h = id_copy(3, ids.at[head], ids.at[head], cross)

    @pl.when(jnp.logical_not(last))
    def _():
        id_y.start()

    @pl.loop(0, HELD)
    def _(i):
        own(i, 4, ld_sem).wait()

        @pl.when(jnp.logical_not(last))
        def _():
            y_copy(i).start()

    @pl.loop(HELD, steps)
    def _(i):
        own(i, 4, ld_sem).wait()

    @pl.when(chip == 1)
    def _():
        early_x().start()

    @pl.when(chip == 0)
    def _():
        x_copy(0).start()

    id_y.wait_recv()
    id_x.start()

    @pl.when(chip == 0)
    def _():
        @pl.loop(1, AHEAD)
        def _(i):
            x_copy(i).start()

    def relay_y(i):
        y_copy(i).wait_recv()
        out_i = i + AHEAD * (1 - chip)

        @pl.when(x_sends(out_i))
        def _():
            x_copy(out_i).start()

        @pl.when((i == EARLY) & (chip == 1) & first)
        def _():
            x_copy(i, e_sem.at[2]).start()

        a_copy(i).start()

    def relay_x(i):
        x_copy(i).wait_recv()
        b_copy(i).start()

    def arrive(i):
        a_copy(i).wait_recv()
        b_copy(i).wait_recv()

    def ids_of(t, slot):
        place = 2 * chip + core + slot
        r = lax.rem(place, 4)
        return ids[t, lax.rem(r, 2), r // 2, place // 4]

    def make_bias():
        mine = [
            jnp.swapaxes(jnp.broadcast_to(ids_of(t, 4), (half, half)), 0, 1)
            for t in range(2)
        ]
        row = lax.broadcasted_iota(jnp.int32, (half, half), 0)
        lane = lax.broadcasted_iota(jnp.int32, (half, half), 1)
        for top in range(2):
            for slot in range(5):
                for t in range(2):
                    key_pos = slot * rows + t * half - 4 * rows
                    gap = row + (top * half - key_pos) - lane
                    visible = (
                        (mine[top] == ids_of(t, slot))
                        & (gap >= 0) & (gap < WINDOW)
                        & (lane + (s * rows + key_pos) >= 0)
                    )
                    bias[pl.ds(top * half, half), pl.ds(slot * rows + t * half, half)] = (
                        jnp.where(visible, 0.0, -1e30)
                    )

    def weigh(h):
        load_q(h).wait()
        for t in range(2):
            scores = lax.dot_general(
                qbuf[h, :, pl.ds(t * HEAD_WIDTH, HEAD_WIDTH)], kv[0, h],
                (((1,), (1,)), ((), ())), preferred_element_type=jnp.float32)
            scores = scores * (SCALE * LOG2E) + bias[...]
            top = jnp.max(scores, axis=1, keepdims=True)
            weights = jnp.exp2(scores - top)
            l_buf[lax.rem(h, 2), t] = jnp.broadcast_to(jnp.sum(weights, axis=1, keepdims=True), (rows, HEAD_WIDTH))
            p_buf[lax.rem(h, 2), t] = weights.astype(jnp.bfloat16)

    def mix(h):
        for t in range(2):
            mixed = jnp.dot(p_buf[lax.rem(h, 2), t], kv[1, h], preferred_element_type=jnp.float32)
            out[:, pl.ds(pl.multiple_of(h * 256 + t * HEAD_WIDTH, HEAD_WIDTH), HEAD_WIDTH)] = (
                mixed / l_buf[lax.rem(h, 2), t]).astype(jnp.bfloat16)

    def step(i, state):
        relayed, done = state
        relay_y(i)

        @pl.when(i == 0)
        def _():
            id_x.wait_recv()
            id_c.start()

            @pl.when(chip == 0)
            def _():
                early_x().wait_recv()

            @pl.when(jnp.logical_not(last))
            def _():
                @pl.when(chip == 0)
                def _():
                    early_y().start()

                @pl.loop(HELD, steps)
                def _(j):
                    y_copy(j).start()

        @pl.when(i == 1)
        def _():
            id_c.wait_recv()
            id_h.start()

        relay_to = jnp.maximum(i + 1 - X_LAG, 0) + i // (steps - 4) + i // (steps - 3)
        relay_to = relay_to + (X_LAG - 2) * (i // (steps - 2))
        done_to = (jnp.maximum(i + 1 - UNIT_LAG, 0) + i // (steps - 4) + i // (steps - 3)
                   + (UNIT_LAG - 2) * (i // (steps - 1)))

        @pl.loop(relayed, relay_to)
        def _(j):
            relay_x(j)

        @pl.loop(done, done_to)
        def _(j):
            arrive(j)
            c, h = unit(j)

            @pl.when(j == 0)
            def _():
                id_h.wait_recv()
                make_bias()

            @pl.when(c == 0)
            def _():
                weigh(h)

            @pl.when(c == 1)
            def _():
                mix(h)

        return relay_to, done_to

    lax.fori_loop(0, steps, step, (jnp.int32(0), jnp.int32(0)))

    def sent(sem, peer):
        shard = kv.at[:, :, pl.ds(4 * rows, rows), :]
        remote(shard, shard, sem, y_recv.at[0], peer).wait_send()

    for copy in (id_x, id_c, id_h):
        copy.wait_send()
    sent(x_send, x_peer)
    sent(a_send, c_peer)
    sent(b_send, c_peer)

    @pl.when(jnp.logical_not(last))
    def _():
        id_y.wait_send()
        sent(y_send, y_next)

        @pl.when(chip == 0)
        def _():
            early_y().wait_send()

    @pl.when((chip == 1) & first)
    def _():
        x_copy(EARLY, e_sem.at[2]).wait_send()


def body(queries, keys, values, segment_ids):
    rows, width = keys.shape
    heads = width // HEAD_WIDTH
    n_seq = lax.axis_size("seq")
    half = segment_ids.shape[0]
    steps = 2 * heads
    dma = pltpu.SemaphoreType.DMA
    return pl.pallas_call(
        functools.partial(kernel, n_seq),
        out_shape=pltpu.VMEM(queries.shape, queries.dtype),
        in_specs=[pl.BlockSpec(memory_space=pl.ANY)] * 4,
        out_specs=pl.BlockSpec(memory_space=pltpu.VMEM),
        scratch_shapes=[
            pltpu.VMEM((2, heads, 5 * rows, HEAD_WIDTH), jnp.bfloat16),
            pltpu.VMEM((rows, HEAD_WIDTH), jnp.bfloat16),
            pltpu.VMEM((heads, rows, 256), jnp.bfloat16),
            pltpu.VMEM((2, 2, 2, 2, 1, half), jnp.int32),
            pltpu.VMEM((rows, 5 * rows), jnp.float32),
            pltpu.VMEM((2, 2, rows, 5 * rows), jnp.bfloat16),
            pltpu.VMEM((2, 2, rows, HEAD_WIDTH), jnp.float32),
            dma((steps,)), dma((heads,)), dma, dma((3,)), dma((4,)), dma((4,)),
            dma, dma((steps,)), dma, dma((steps,)),
            dma, dma((steps,)), dma, dma((steps,)),
        ],
        compiler_params=pltpu.CompilerParams(collective_id=0, has_side_effects=True),
    )(queries, keys, values, segment_ids.reshape(1, half))


def solution(mesh):
    in_specs = (P("seq", "head"), P("seq", "head"), P("seq", "head"), P(("seq", "head")))
    out_specs = P("seq", "head")
    return jax.shard_map(body, mesh=mesh, in_specs=in_specs, out_specs=out_specs, check_vma=False)
```

time: 38.1 us -> 37.5 us (0.984); the launches traced: 37.6 us -> 37.4 us
  no operation moved by 1% of the time
where the time goes in v3:
time: 37.5 us; the launch traced here: 37.4 us
  Pallas kernels  36.5 us (97%)
  local copies, waits for them, and re-layouts  0.97 us (3%)
    pallas_call x1, Pallas kernels, body(): pl.pallas_call(functools.partial(kernel, n_seq), out_shape=pltpu.VMEM(que...  36.5 us
    unnamed x1, local copies, waits for them, and re-layouts  0.97 us

profile of v3, /device:TPU:192, one launch (start us, length us, event | category | flops | bytes accessed | tf_op | source)
XLA Modules:
  0.0 37.4 jit_solution(12511380716592384209)
XLA Ops:
  0.0 36.5 %shard_map.46 = bf16[256,2048]{1,0:T(8,128)(2,1)S(1)} custom-call(bf16[256,2048]{1,0:T(8,128)(2,1)} %q_hbm.1, bf16[256,1024]{1,0:T(8,128)(2,1)} %k_hbm.1, bf16[256,1024]{1,0:T(8,128)(2,1)} %v_hbm.1, s32[1,128]{1,0:T(1,128)} %bitcast.1), custom_call_target="tpu_custom_call" | custom-call | tf_op jit(solution)/shard_map/pallas_call | solution.py:336
  36.5 1.0 %copy.6 = bf16[256,2048]{1,0:T(8,128)(2,1)} copy(bf16[256,2048]{1,0:T(8,128)(2,1)S(1)} %shard_map.46) | data formatting | bytes 2097152

commit v4 on v3

--- a/solution.py
+++ b/solution.py
@@ -14,8 +14,8 @@
 MESH = pl.DeviceIdType.MESH
 X_LAG = 2
 UNIT_LAG = 4
-EARLY = 14
-HELD = 13
+EARLY = 13
+HELD = 12
 AHEAD = 4
 
 
@@ -273,8 +273,9 @@
 
         relay_to = jnp.maximum(i + 1 - X_LAG, 0) + i // (steps - 4) + i // (steps - 3)
         relay_to = relay_to + (X_LAG - 2) * (i // (steps - 2))
-        done_to = (jnp.maximum(i + 1 - UNIT_LAG, 0) + i // (steps - 4) + i // (steps - 3)
-                   + (UNIT_LAG - 2) * (i // (steps - 1)))
+        done_to = (jnp.maximum(i + 1 - UNIT_LAG, 0)
+                   + (1 - chip) * (i // (steps - 6) + i // (steps - 3) - 2 * (i // (steps - 1)))
+                   + UNIT_LAG * (i // (steps - 1)))
 
         @pl.loop(relayed, relay_to)
         def _(j):

time: 37.5 us -> 36.9 us (0.984)
  Pallas kernels: 36.5 us -> 35.8 us
    pallas_call x1, Pallas kernels: 36.5 us -> 35.8 us  [body(): pl.pallas_call(functools.partial(kernel, n_seq), out_shape=pltpu.VMEM(que...]
where the time goes in v4:
time: 36.9 us; the launch traced here: 36.8 us
  Pallas kernels  35.8 us (97%)
  local copies, waits for them, and re-layouts  0.97 us (3%)
    pallas_call x1, Pallas kernels, body(): pl.pallas_call(functools.partial(kernel, n_seq), out_shape=pltpu.VMEM(que...  35.8 us
    unnamed x1, local copies, waits for them, and re-layouts  0.97 us

profile of v4, /device:TPU:192, one launch (start us, length us, event | category | flops | bytes accessed | tf_op | source)
XLA Modules:
  0.0 36.8 jit_solution(12697798665286152823)
XLA Ops:
  0.0 35.8 %shard_map.46 = bf16[256,2048]{1,0:T(8,128)(2,1)S(1)} custom-call(bf16[256,2048]{1,0:T(8,128)(2,1)} %q_hbm.1, bf16[256,1024]{1,0:T(8,128)(2,1)} %k_hbm.1, bf16[256,1024]{1,0:T(8,128)(2,1)} %v_hbm.1, s32[1,128]{1,0:T(1,128)} %bitcast.1), custom_call_target="tpu_custom_call" | custom-call | tf_op jit(solution)/shard_map/pallas_call | solution.py:337
  35.8 1.0 %copy.6 = bf16[256,2048]{1,0:T(8,128)(2,1)} copy(bf16[256,2048]{1,0:T(8,128)(2,1)S(1)} %shard_map.46) | data formatting | bytes 2097152

commit v5 on v4

--- a/solution.py
+++ b/solution.py
@@ -274,7 +274,7 @@
         relay_to = jnp.maximum(i + 1 - X_LAG, 0) + i // (steps - 4) + i // (steps - 3)
         relay_to = relay_to + (X_LAG - 2) * (i // (steps - 2))
         done_to = (jnp.maximum(i + 1 - UNIT_LAG, 0)
-                   + (1 - chip) * (i // (steps - 6) + i // (steps - 3) - 2 * (i // (steps - 1)))
+                   + (1 - chip) * (i // (steps - 8) + i // (steps - 3) - 2 * (i // (steps - 1)))
                    + UNIT_LAG * (i // (steps - 1)))
 
         @pl.loop(relayed, relay_to)

time: 36.9 us -> 36.9 us (level)
  no operation moved by 1% of the time
where the time goes in v5:
time: 36.9 us; the launch traced here: 36.8 us
  Pallas kernels  35.8 us (97%)
  local copies, waits for them, and re-layouts  0.97 us (3%)
    pallas_call x1, Pallas kernels, body(): pl.pallas_call(functools.partial(kernel, n_seq), out_shape=pltpu.VMEM(que...  35.8 us
    unnamed x1, local copies, waits for them, and re-layouts  0.97 us

profile of v5, /device:TPU:192, one launch (start us, length us, event | category | flops | bytes accessed | tf_op | source)
XLA Modules:
  0.0 36.8 jit_solution(15190512040973107142)
XLA Ops:
  0.0 35.8 %shard_map.46 = bf16[256,2048]{1,0:T(8,128)(2,1)S(1)} custom-call(bf16[256,2048]{1,0:T(8,128)(2,1)} %q_hbm.1, bf16[256,1024]{1,0:T(8,128)(2,1)} %k_hbm.1, bf16[256,1024]{1,0:T(8,128)(2,1)} %v_hbm.1, s32[1,128]{1,0:T(1,128)} %bitcast.1), custom_call_target="tpu_custom_call" | custom-call | tf_op jit(solution)/shard_map/pallas_call | solution.py:337
  35.8 1.0 %copy.6 = bf16[256,2048]{1,0:T(8,128)(2,1)} copy(bf16[256,2048]{1,0:T(8,128)(2,1)S(1)} %shard_map.46) | data formatting | bytes 2097152
